TPU v7x, 128 devices: a whole 4x4x4 slice. The times are simulated.
128 devices in a mesh: section: 8 (over z, x_hi), expert: 16 (over x_lo, y, core).
Axes of the slice: x: 4 (x_hi: 2, x_lo: 2; x = x_hi * 2 + x_lo), y: 4, z: 4, core: 2. Of those that a mesh axis runs over, the one named last changes fastest.
Arguments:
- layer_inputs: bfloat16 [8, 2, 1024, 2560], P('section', None, 'expert'), may hold values from -6 to 6
- norm_gain: float32 [8, 2560], P('section'), may hold values from 0.1 to 1.9
- routing: int32 [8, 2, 1024, 6], P('section', None, 'expert'), may hold values from 0 to 15, all different within a row; in each aligned block of 64 rows (0 to 63, 64 to 127, ..., all dimensions but the last counted through in order) at most 40 rows name the same one
- route_weight: float32 [8, 2, 1024, 6], P('section', None, 'expert'), may hold values from 0.05 to 0.6
- w_gate: bfloat16 [8, 16, 2560, 768], P('section', 'expert'), may hold values from -0.125 to 0.125
- w_up: bfloat16 [8, 16, 2560, 768], P('section', 'expert'), may hold values from -0.125 to 0.125
- w_down: bfloat16 [8, 16, 768, 2560], P('section', 'expert'), may hold values from -0.21875 to 0.21875
- top_grad: bfloat16 [2, 1024, 2560], P(None, 'expert'), may hold values from -6 to 6
Outputs:
- layer_grads: bfloat16 [8, 2, 1024, 2560], P('section', None, 'expert')
Inputs may be any that keep to these rules, and one draw needn't show every extreme that they name: `routing`: in each aligned block of 64 rows (one device's tokens of one micro-batch in one layer) no expert is named by more than 40 rows, a bound that some block reaches.
All inputs are finite; a program needn't handle non-finite values.
Results may differ from a plain program's by a relative error of at most 0.025.
Values may be sent and summed in bfloat16 or wider, within the bound.
A program may use at most 128 MiB of HBM per device.

v0:
```python
import jax
import jax.numpy as jnp
from jax import lax
from jax.sharding import PartitionSpec as P

EPSILON = 1e-06


def from_behind(array, axis, by):
    count = lax.axis_size(axis)
    return lax.ppermute(array, axis, [(i, (i + by) % count) for i in range(count)])


def norm_parts(inputs, gain_row):
    values = inputs.astype(jnp.float32)
    scale = lax.rsqrt(jnp.mean(values * values, axis=-1, keepdims=True) + EPSILON)
    normed = (values * scale * gain_row).astype(jnp.bfloat16)
    return (values, scale, normed)


def norm_back(values, scale, gain_row, upstream):
    scaled = gain_row * upstream
    return scale * scaled - values * scale**3 * jnp.mean(values * scaled, axis=-1, keepdims=True)


def slot_numbers(chosen, experts, capacity):
    flat = chosen.reshape(-1)
    onehot = (flat[:, None] == jnp.arange(experts, dtype=jnp.int32)[None, :]).astype(jnp.int32)
    earlier = jnp.cumsum(onehot, axis=0) - onehot
    ranks = jnp.sum(earlier * onehot, axis=1)
    return flat * capacity + ranks


def per_device(layer_inputs, norm_gain, routing, route_weight, w_gate, w_up, w_down, top_grad):
    sections = lax.axis_size("section")
    experts = lax.axis_size("expert")
    section_index = lax.axis_index("section")
    chain_depth = sections - 1 - (section_index - sections // 2) % sections
    micro_count = layer_inputs.shape[1]
    token_count = layer_inputs.shape[2]
    top_count = routing.shape[3]
    width = layer_inputs.shape[3]
    capacity = min(token_count, 5 * token_count * top_count // (3 * experts))
    gain_row = norm_gain[0]
    gate_mat = w_gate[0, 0]
    up_mat = w_up[0, 0]
    down_mat = w_down[0, 0]
    values, scale, normed = norm_parts(layer_inputs[0], gain_row)
    slot_table = jnp.stack(
        [slot_numbers(routing[0, index], experts, capacity) for index in range(micro_count)]
    )
    owner_rows = jnp.arange(token_count * top_count, dtype=jnp.int32) // top_count

    def owner_table(slots):
        return jnp.full((experts * capacity,), token_count, jnp.int32).at[slots].set(owner_rows)

    def fill_buffer(table, rows):
        padded = jnp.concatenate([rows, jnp.zeros((1, width), rows.dtype)], 0)
        return padded[table].reshape(experts, capacity, width)

    def project(received):
        pre_gate = jnp.einsum("ncd,dh->nch", received, gate_mat, preferred_element_type=jnp.float32)
        pre_up = jnp.einsum("ncd,dh->nch", received, up_mat, preferred_element_type=jnp.float32)
        return (pre_gate, pre_up)

    def finish(grads_in, pre_gate, pre_up):
        hidden_grad = jnp.einsum(
            "ncd,hd->nch", grads_in, down_mat, preferred_element_type=jnp.float32
        )
        sigma = jax.nn.sigmoid(pre_gate)
        grad_gate = (hidden_grad * pre_up * sigma * (1.0 + pre_gate * (1.0 - sigma))).astype(
            jnp.bfloat16
        )
        grad_upper = (hidden_grad * pre_gate * sigma).astype(jnp.bfloat16)
        result = jnp.einsum("nch,dh->ncd", grad_gate, gate_mat, preferred_element_type=jnp.float32)
        result = result + jnp.einsum(
            "nch,dh->ncd", grad_upper, up_mat, preferred_element_type=jnp.float32
        )
        return result.astype(jnp.bfloat16)

    owners_all = jnp.stack(
        [owner_table(slots) for slots in [slot_table[index] for index in range(micro_count)]]
    )

    def tick(tick_number, carry):
        arriving, results = carry
        offset = tick_number - chain_depth
        active = (offset >= 0) & (offset < micro_count)
        micro_id = jnp.clip(offset, 0, micro_count - 1)
        incoming = jnp.where(chain_depth == 0, top_grad[micro_id], arriving)
        table = owners_all[micro_id]
        grad_buffer = fill_buffer(table, incoming)
        row_buffer = fill_buffer(table, normed[micro_id])

        def compute_joint(pair):
            rows_recv, grads_recv = pair
            pre_gate, pre_up = project(rows_recv)
            return finish(grads_recv, pre_gate, pre_up)

        def empty_joint(pair):
            return jnp.zeros(pair[1].shape, jnp.bfloat16)

        result = lax.cond(
            active,
            compute_joint,
            empty_joint,
            (
                lax.all_to_all(row_buffer, "expert", split_axis=0, concat_axis=0, tiled=True),
                lax.all_to_all(grad_buffer, "expert", split_axis=0, concat_axis=0, tiled=True),
            ),
        )
        returned = lax.all_to_all(result, "expert", split_axis=0, concat_axis=0, tiled=True)
        picked = returned.reshape(experts * capacity, width)[slot_table[micro_id]]
        picked = picked.reshape(token_count, top_count, width).astype(jnp.float32)
        upstream = jnp.einsum(
            "tkd,tk->td", picked, route_weight[0, micro_id], precision=lax.Precision.HIGHEST
        )
        change = norm_back(values[micro_id], scale[micro_id], gain_row, upstream)
        fresh = (incoming.astype(jnp.float32) + change).astype(jnp.bfloat16)
        fresh = jnp.where(active, fresh, jnp.zeros_like(fresh))
        updated = lax.dynamic_update_index_in_dim(results, fresh, micro_id, 0)
        results = jnp.where(active, updated, results)
        arriving = from_behind(fresh, "section", -1)
        return (arriving, results)

    start = (
        jnp.zeros((token_count, width), jnp.bfloat16),
        jnp.zeros((micro_count, token_count, width), jnp.bfloat16),
    )
    final_carry = lax.fori_loop(0, sections + micro_count - 1, tick, start)
    return final_carry[1][None]


def solution(mesh):
    placed = (
        P("section", None, "expert", None),
        P("section", None),
        P("section", None, "expert", None),
        P("section", None, "expert", None),
        P("section", "expert", None, None),
        P("section", "expert", None, None),
        P("section", "expert", None, None),
        P(None, "expert", None),
    )
    return jax.shard_map(
        per_device,
        mesh=mesh,
        in_specs=placed,
        out_specs=P("section", None, "expert", None),
        check_vma=False,
    )
```

profile of v0, /device:TPU:90, one launch (start us, length us, event | category | flops | bytes accessed | tf_op | source)
XLA Modules:
  0.0 1999.2 jit_solution(13164858424503095734)
XLA Ops:
  17.2 1982.0 %while.16 = (s32[]{:T(128)}, bf16[64,2560]{1,0:T(8,128)(2,1)S(1)}, bf16[2,64,2560]{2,1,0:T(8,128)(2,1)}, s32[]{:T(128)}, pred[]{:T(512)}, /*index=5*/bf16[2,64,2...) while((s32[]{:T(128)}, bf16[64,2560]{1,0:T(8,128)(2,1)S(1)}, ...), condition=%wide.region_13.14_spmd, body=%wide.region_9.13_spmd.sunk | while | flops 12608148480 | bytes 160991440 | solution.py:130
  34.5 42.0 %all-to-all-done = bf16[16,40,2560]{2,1,0:T(8,128)(2,1)} async-done(((bf16[16,40,2560]{2,1,0:T(8,128)(2,1)}), bf16[16,40,2560]{2,1,0:T(8,128)(2,1)}, u32[]{:S(2)}, u32[]{:S(2)}) %all-to-all-start) | async-done | bytes 3276832 | tf_op jit(solution)/shard_map/while/body/eval_jaxpr/all_to_all | solution.py:109
  81.9 47.2 %all-to-all-done.1 = bf16[16,40,2560]{2,1,0:T(8,128)(2,1)S(1)} async-done(((bf16[16,40,2560]{2,1,0:T(8,128)(2,1)}), bf16[16,40,2560]{2,1,0:T(8,128)(2,1)S(1)}, u32[]{:S(2)}, u32[]{:S(2)}) %all-to-all-start.1) | async-done | bytes 3276832 | tf_op jit(solution)/shard_map/while/body/eval_jaxpr/all_to_all | solution.py:108
  136.7 47.0 %all-to-all-done.2 = bf16[16,40,2560]{2,1,0:T(8,128)(2,1)S(1)} async-done(((bf16[16,40,2560]{2,1,0:T(8,128)(2,1)}), bf16[16,40,2560]{2,1,0:T(8,128)(2,1)S(1)}, u32[]{:S(2)}, u32[]{:S(2)}) %all-to-all-start.2) | async-done | bytes 3276832 | tf_op jit(solution)/shard_map/while/body/eval_jaxpr/all_to_all | solution.py:112
  192.5 36.1 %collective-permute-start = (bf16[64,2560]{1,0:T(8,128)(2,1)S(1)}, bf16[64,2560]{1,0:T(8,128)(2,1)S(1)}, u32[]{:S(2)}, u32[]{:S(2)}) collective-permute-start(bf16[64,2560]{1,0:T(8,128)(2,1)S(1)} %get-tuple-element.529), channel_id=1, source_target_pairs={{0,112},{16,0},{32,16},{48,32},{64,48},{80,64},{96,80},{112,96},{1... | collective-permute-start | bytes 983048 | tf_op jit(solution)/shard_map/while/body/eval_jaxpr/ppermute | solution.py:11
  228.6 7.5 collective-permute-done
  253.1 42.0 %all-to-all-done = bf16[16,40,2560]{2,1,0:T(8,128)(2,1)} async-done(((bf16[16,40,2560]{2,1,0:T(8,128)(2,1)}), bf16[16,40,2560]{2,1,0:T(8,128)(2,1)}, u32[]{:S(2)}, u32[]{:S(2)}) %all-to-all-start) | async-done | bytes 3276832 | tf_op jit(solution)/shard_map/while/body/eval_jaxpr/all_to_all | solution.py:109
  300.5 47.2 %all-to-all-done.1 = bf16[16,40,2560]{2,1,0:T(8,128)(2,1)S(1)} async-done(((bf16[16,40,2560]{2,1,0:T(8,128)(2,1)}), bf16[16,40,2560]{2,1,0:T(8,128)(2,1)S(1)}, u32[]{:S(2)}, u32[]{:S(2)}) %all-to-all-start.1) | async-done | bytes 3276832 | tf_op jit(solution)/shard_map/while/body/eval_jaxpr/all_to_all | solution.py:108
  355.3 47.0 %all-to-all-done.2 = bf16[16,40,2560]{2,1,0:T(8,128)(2,1)S(1)} async-done(((bf16[16,40,2560]{2,1,0:T(8,128)(2,1)}), bf16[16,40,2560]{2,1,0:T(8,128)(2,1)S(1)}, u32[]{:S(2)}, u32[]{:S(2)}) %all-to-all-start.2) | async-done | bytes 3276832 | tf_op jit(solution)/shard_map/while/body/eval_jaxpr/all_to_all | solution.py:112
  411.1 39.4 %collective-permute-start = (bf16[64,2560]{1,0:T(8,128)(2,1)S(1)}, bf16[64,2560]{1,0:T(8,128)(2,1)S(1)}, u32[]{:S(2)}, u32[]{:S(2)}) collective-permute-start(bf16[64,2560]{1,0:T(8,128)(2,1)S(1)} %get-tuple-element.529), channel_id=1, source_target_pairs={{0,112},{16,0},{32,16},{48,32},{64,48},{80,64},{96,80},{112,96},{1... | collective-permute-start | bytes 983048 | tf_op jit(solution)/shard_map/while/body/eval_jaxpr/ppermute | solution.py:11
  450.5 7.5 collective-permute-done
  475.0 42.0 %all-to-all-done = bf16[16,40,2560]{2,1,0:T(8,128)(2,1)} async-done(((bf16[16,40,2560]{2,1,0:T(8,128)(2,1)}), bf16[16,40,2560]{2,1,0:T(8,128)(2,1)}, u32[]{:S(2)}, u32[]{:S(2)}) %all-to-all-start) | async-done | bytes 3276832 | tf_op jit(solution)/shard_map/while/body/eval_jaxpr/all_to_all | solution.py:109
  522.4 47.2 %all-to-all-done.1 = bf16[16,40,2560]{2,1,0:T(8,128)(2,1)S(1)} async-done(((bf16[16,40,2560]{2,1,0:T(8,128)(2,1)}), bf16[16,40,2560]{2,1,0:T(8,128)(2,1)S(1)}, u32[]{:S(2)}, u32[]{:S(2)}) %all-to-all-start.1) | async-done | bytes 3276832 | tf_op jit(solution)/shard_map/while/body/eval_jaxpr/all_to_all | solution.py:108
  577.1 47.0 %all-to-all-done.2 = bf16[16,40,2560]{2,1,0:T(8,128)(2,1)S(1)} async-done(((bf16[16,40,2560]{2,1,0:T(8,128)(2,1)}), bf16[16,40,2560]{2,1,0:T(8,128)(2,1)S(1)}, u32[]{:S(2)}, u32[]{:S(2)}) %all-to-all-start.2) | async-done | bytes 3276832 | tf_op jit(solution)/shard_map/while/body/eval_jaxpr/all_to_all | solution.py:112
  637.9 7.5 collective-permute-done
  662.4 42.0 %all-to-all-done = bf16[16,40,2560]{2,1,0:T(8,128)(2,1)} async-done(((bf16[16,40,2560]{2,1,0:T(8,128)(2,1)}), bf16[16,40,2560]{2,1,0:T(8,128)(2,1)}, u32[]{:S(2)}, u32[]{:S(2)}) %all-to-all-start) | async-done | bytes 3276832 | tf_op jit(solution)/shard_map/while/body/eval_jaxpr/all_to_all | solution.py:109
  709.8 47.2 %all-to-all-done.1 = bf16[16,40,2560]{2,1,0:T(8,128)(2,1)S(1)} async-done(((bf16[16,40,2560]{2,1,0:T(8,128)(2,1)}), bf16[16,40,2560]{2,1,0:T(8,128)(2,1)S(1)}, u32[]{:S(2)}, u32[]{:S(2)}) %all-to-all-start.1) | async-done | bytes 3276832 | tf_op jit(solution)/shard_map/while/body/eval_jaxpr/all_to_all | solution.py:108
  764.6 47.0 %all-to-all-done.2 = bf16[16,40,2560]{2,1,0:T(8,128)(2,1)S(1)} async-done(((bf16[16,40,2560]{2,1,0:T(8,128)(2,1)}), bf16[16,40,2560]{2,1,0:T(8,128)(2,1)S(1)}, u32[]{:S(2)}, u32[]{:S(2)}) %all-to-all-start.2) | async-done | bytes 3276832 | tf_op jit(solution)/shard_map/while/body/eval_jaxpr/all_to_all | solution.py:112
  820.4 33.9 %collective-permute-start = (bf16[64,2560]{1,0:T(8,128)(2,1)S(1)}, bf16[64,2560]{1,0:T(8,128)(2,1)S(1)}, u32[]{:S(2)}, u32[]{:S(2)}) collective-permute-start(bf16[64,2560]{1,0:T(8,128)(2,1)S(1)} %get-tuple-element.529), channel_id=1, source_target_pairs={{0,112},{16,0},{32,16},{48,32},{64,48},{80,64},{96,80},{112,96},{1... | collective-permute-start | bytes 983048 | tf_op jit(solution)/shard_map/while/body/eval_jaxpr/ppermute | solution.py:11
  854.3 7.5 collective-permute-done
  878.7 42.0 %all-to-all-done = bf16[16,40,2560]{2,1,0:T(8,128)(2,1)} async-done(((bf16[16,40,2560]{2,1,0:T(8,128)(2,1)}), bf16[16,40,2560]{2,1,0:T(8,128)(2,1)}, u32[]{:S(2)}, u32[]{:S(2)}) %all-to-all-start) | async-done | bytes 3276832 | tf_op jit(solution)/shard_map/while/body/eval_jaxpr/all_to_all | solution.py:109
  926.1 47.2 %all-to-all-done.1 = bf16[16,40,2560]{2,1,0:T(8,128)(2,1)S(1)} async-done(((bf16[16,40,2560]{2,1,0:T(8,128)(2,1)}), bf16[16,40,2560]{2,1,0:T(8,128)(2,1)S(1)}, u32[]{:S(2)}, u32[]{:S(2)}) %all-to-all-start.1) | async-done | bytes 3276832 | tf_op jit(solution)/shard_map/while/body/eval_jaxpr/all_to_all | solution.py:108
  980.9 47.0 %all-to-all-done.2 = bf16[16,40,2560]{2,1,0:T(8,128)(2,1)S(1)} async-done(((bf16[16,40,2560]{2,1,0:T(8,128)(2,1)}), bf16[16,40,2560]{2,1,0:T(8,128)(2,1)S(1)}, u32[]{:S(2)}, u32[]{:S(2)}) %all-to-all-start.2) | async-done | bytes 3276832 | tf_op jit(solution)/shard_map/while/body/eval_jaxpr/all_to_all | solution.py:112
  1041.7 7.5 collective-permute-done
  1066.2 42.0 %all-to-all-done = bf16[16,40,2560]{2,1,0:T(8,128)(2,1)} async-done(((bf16[16,40,2560]{2,1,0:T(8,128)(2,1)}), bf16[16,40,2560]{2,1,0:T(8,128)(2,1)}, u32[]{:S(2)}, u32[]{:S(2)}) %all-to-all-start) | async-done | bytes 3276832 | tf_op jit(solution)/shard_map/while/body/eval_jaxpr/all_to_all | solution.py:109
  1113.6 47.2 %all-to-all-done.1 = bf16[16,40,2560]{2,1,0:T(8,128)(2,1)S(1)} async-done(((bf16[16,40,2560]{2,1,0:T(8,128)(2,1)}), bf16[16,40,2560]{2,1,0:T(8,128)(2,1)S(1)}, u32[]{:S(2)}, u32[]{:S(2)}) %all-to-all-start.1) | async-done | bytes 3276832 | tf_op jit(solution)/shard_map/while/body/eval_jaxpr/all_to_all | solution.py:108
  1168.3 47.0 %all-to-all-done.2 = bf16[16,40,2560]{2,1,0:T(8,128)(2,1)S(1)} async-done(((bf16[16,40,2560]{2,1,0:T(8,128)(2,1)}), bf16[16,40,2560]{2,1,0:T(8,128)(2,1)S(1)}, u32[]{:S(2)}, u32[]{:S(2)}) %all-to-all-start.2) | async-done | bytes 3276832 | tf_op jit(solution)/shard_map/while/body/eval_jaxpr/all_to_all | solution.py:112
  1224.2 34.8 %collective-permute-start = (bf16[64,2560]{1,0:T(8,128)(2,1)S(1)}, bf16[64,2560]{1,0:T(8,128)(2,1)S(1)}, u32[]{:S(2)}, u32[]{:S(2)}) collective-permute-start(bf16[64,2560]{1,0:T(8,128)(2,1)S(1)} %get-tuple-element.529), channel_id=1, source_target_pairs={{0,112},{16,0},{32,16},{48,32},{64,48},{80,64},{96,80},{112,96},{1... | collective-permute-start | bytes 983048 | tf_op jit(solution)/shard_map/while/body/eval_jaxpr/ppermute | solution.py:11
  1259.0 7.5 collective-permute-done
  1283.4 42.0 %all-to-all-done = bf16[16,40,2560]{2,1,0:T(8,128)(2,1)} async-done(((bf16[16,40,2560]{2,1,0:T(8,128)(2,1)}), bf16[16,40,2560]{2,1,0:T(8,128)(2,1)}, u32[]{:S(2)}, u32[]{:S(2)}) %all-to-all-start) | async-done | bytes 3276832 | tf_op jit(solution)/shard_map/while/body/eval_jaxpr/all_to_all | solution.py:109
  1330.8 47.2 %all-to-all-done.1 = bf16[16,40,2560]{2,1,0:T(8,128)(2,1)S(1)} async-done(((bf16[16,40,2560]{2,1,0:T(8,128)(2,1)}), bf16[16,40,2560]{2,1,0:T(8,128)(2,1)S(1)}, u32[]{:S(2)}, u32[]{:S(2)}) %all-to-all-start.1) | async-done | bytes 3276832 | tf_op jit(solution)/shard_map/while/body/eval_jaxpr/all_to_all | solution.py:108
  1385.6 47.0 %all-to-all-done.2 = bf16[16,40,2560]{2,1,0:T(8,128)(2,1)S(1)} async-done(((bf16[16,40,2560]{2,1,0:T(8,128)(2,1)}), bf16[16,40,2560]{2,1,0:T(8,128)(2,1)S(1)}, u32[]{:S(2)}, u32[]{:S(2)}) %all-to-all-start.2) | async-done | bytes 3276832 | tf_op jit(solution)/shard_map/while/body/eval_jaxpr/all_to_all | solution.py:112
  1446.4 108.8 %collective-permute-done = bf16[64,2560]{1,0:T(8,128)(2,1)S(1)} collective-permute-done((bf16[64,2560]{1,0:T(8,128)(2,1)S(1)}, bf16[64,2560]{1,0:T(8,128)(2,1)S(1)}, u32[]{:S(2)}, u32[]{:S(2)}) %collective-permute-start) | collective-permute-done | bytes 327712 | tf_op jit(solution)/shard_map/while/body/eval_jaxpr/ppermute | solution.py:11
  1572.1 42.0 %all-to-all-done = bf16[16,40,2560]{2,1,0:T(8,128)(2,1)} async-done(((bf16[16,40,2560]{2,1,0:T(8,128)(2,1)}), bf16[16,40,2560]{2,1,0:T(8,128)(2,1)}, u32[]{:S(2)}, u32[]{:S(2)}) %all-to-all-start) | async-done | bytes 3276832 | tf_op jit(solution)/shard_map/while/body/eval_jaxpr/all_to_all | solution.py:109
  1619.5 47.2 %all-to-all-done.1 = bf16[16,40,2560]{2,1,0:T(8,128)(2,1)S(1)} async-done(((bf16[16,40,2560]{2,1,0:T(8,128)(2,1)}), bf16[16,40,2560]{2,1,0:T(8,128)(2,1)S(1)}, u32[]{:S(2)}, u32[]{:S(2)}) %all-to-all-start.1) | async-done | bytes 3276832 | tf_op jit(solution)/shard_map/while/body/eval_jaxpr/all_to_all | solution.py:108
  1666.8 34.6 %conditional.2 = (bf16[16,40,2560]{2,1,0:T(8,128)(2,1)S(1)}) conditional(s32[]{:T(128)} %convert_element_type.87, () %tuple.51, (bf16[16,40,2560]{2,1,0:T(8,128)(2,1)}, bf16[768,2560]{1,0:T(8,128)(2,1)}, bf16[16,40,2560]{2,1,0:T(8,128)(2,1)S(1)}, bf16[2560,768]{1,0:T(8,128)(2,1)}, bf16[2560,768]{1,0:T(8,128)(2,1)}) %tuple.52), branch_computations={%region_10.10_spmd, %region_11.11_spmd} | conditional | flops 12594053120 | bytes 73400360 | solution.py:103
  1666.8 6.3 fusion.2
  1679.1 14.3 fusion
  1693.4 7.9 add_convert_fusion
  1708.7 47.0 %all-to-all-done.2 = bf16[16,40,2560]{2,1,0:T(8,128)(2,1)S(1)} async-done(((bf16[16,40,2560]{2,1,0:T(8,128)(2,1)}), bf16[16,40,2560]{2,1,0:T(8,128)(2,1)S(1)}, u32[]{:S(2)}, u32[]{:S(2)}) %all-to-all-start.2) | async-done | bytes 3276832 | tf_op jit(solution)/shard_map/while/body/eval_jaxpr/all_to_all | solution.py:112
  1764.6 13.6 collective-permute-done
  1795.2 42.0 %all-to-all-done = bf16[16,40,2560]{2,1,0:T(8,128)(2,1)} async-done(((bf16[16,40,2560]{2,1,0:T(8,128)(2,1)}), bf16[16,40,2560]{2,1,0:T(8,128)(2,1)}, u32[]{:S(2)}, u32[]{:S(2)}) %all-to-all-start) | async-done | bytes 3276832 | tf_op jit(solution)/shard_map/while/body/eval_jaxpr/all_to_all | solution.py:109
  1842.6 47.2 %all-to-all-done.1 = bf16[16,40,2560]{2,1,0:T(8,128)(2,1)S(1)} async-done(((bf16[16,40,2560]{2,1,0:T(8,128)(2,1)}), bf16[16,40,2560]{2,1,0:T(8,128)(2,1)S(1)}, u32[]{:S(2)}, u32[]{:S(2)}) %all-to-all-start.1) | async-done | bytes 3276832 | tf_op jit(solution)/shard_map/while/body/eval_jaxpr/all_to_all | solution.py:108
  1889.8 34.6 %conditional.2 = (bf16[16,40,2560]{2,1,0:T(8,128)(2,1)S(1)}) conditional(s32[]{:T(128)} %convert_element_type.87, () %tuple.51, (bf16[16,40,2560]{2,1,0:T(8,128)(2,1)}, bf16[768,2560]{1,0:T(8,128)(2,1)}, bf16[16,40,2560]{2,1,0:T(8,128)(2,1)S(1)}, bf16[2560,768]{1,0:T(8,128)(2,1)}, bf16[2560,768]{1,0:T(8,128)(2,1)}) %tuple.52), branch_computations={%region_10.10_spmd, %region_11.11_spmd} | conditional | flops 12594053120 | bytes 73400360 | solution.py:103
  1902.1 14.3 fusion
  1916.5 7.9 add_convert_fusion
  1931.8 47.0 %all-to-all-done.2 = bf16[16,40,2560]{2,1,0:T(8,128)(2,1)S(1)} async-done(((bf16[16,40,2560]{2,1,0:T(8,128)(2,1)}), bf16[16,40,2560]{2,1,0:T(8,128)(2,1)S(1)}, u32[]{:S(2)}, u32[]{:S(2)}) %all-to-all-start.2) | async-done | bytes 3276832 | tf_op jit(solution)/shard_map/while/body/eval_jaxpr/all_to_all | solution.py:112
  1987.7 11.5 collective-permute-done
  (434 shorter events, 399.0 us)
Async XLA Ops:
  17.4 119.3 %copy-start.9 = (f32[2,64,1]{1,2,0:T(1,128)}, f32[2,64,1]{1,2,0:T(1,128)S(1)}, u32[]{:S(2)}) copy-start(f32[2,64,1]{1,2,0:T(1,128)S(1)} %get-tuple-element.579) | copy-start | bytes 1540 | tf_op jit(solution)/shard_map/while
  23.5 52.9 %all-to-all-start = ((bf16[16,40,2560]{2,1,0:T(8,128)(2,1)}), bf16[16,40,2560]{2,1,0:T(8,128)(2,1)}, u32[]{:S(2)}, u32[]{:S(2)}) async-start(bf16[16,40,2560]{2,1,0:T(8,128)(2,1)} %bitcast.168), calls=%async_computation | async-start | bytes 6553600 | tf_op jit(solution)/shard_map/while/body/eval_jaxpr/all_to_all | solution.py:109
  76.4 52.6 %all-to-all-start.1 = ((bf16[16,40,2560]{2,1,0:T(8,128)(2,1)}), bf16[16,40,2560]{2,1,0:T(8,128)(2,1)S(1)}, u32[]{:S(2)}, u32[]{:S(2)}) async-start(bf16[16,40,2560]{2,1,0:T(8,128)(2,1)} %bitcast.167), calls=%async_computation.1 | async-start | bytes 6553600 | tf_op jit(solution)/shard_map/while/body/eval_jaxpr/all_to_all | solution.py:108
  131.0 52.6 %all-to-all-start.2 = ((bf16[16,40,2560]{2,1,0:T(8,128)(2,1)}), bf16[16,40,2560]{2,1,0:T(8,128)(2,1)S(1)}, u32[]{:S(2)}, u32[]{:S(2)}) async-start(bf16[16,40,2560]{2,1,0:T(8,128)(2,1)} %copy-done), calls=%async_computation.2 | async-start | bytes 6553600 | tf_op jit(solution)/shard_map/while/body/eval_jaxpr/all_to_all | solution.py:112
  192.5 43.7 %collective-permute-start = (bf16[64,2560]{1,0:T(8,128)(2,1)S(1)}, bf16[64,2560]{1,0:T(8,128)(2,1)S(1)}, u32[]{:S(2)}, u32[]{:S(2)}) collective-permute-start(bf16[64,2560]{1,0:T(8,128)(2,1)S(1)} %get-tuple-element.529), channel_id=1, source_target_pairs={{0,112},{16,0},{32,16},{48,32},{64,48},{80,64},{96,80},{112,96},{1... | collective-permute-start | bytes 983048 | tf_op jit(solution)/shard_map/while/body/eval_jaxpr/ppermute | solution.py:11
  236.2 119.1 %copy-start.9 = (f32[2,64,1]{1,2,0:T(1,128)}, f32[2,64,1]{1,2,0:T(1,128)S(1)}, u32[]{:S(2)}) copy-start(f32[2,64,1]{1,2,0:T(1,128)S(1)} %get-tuple-element.579) | copy-start | bytes 1540 | tf_op jit(solution)/shard_map/while
  242.3 52.8 %all-to-all-start = ((bf16[16,40,2560]{2,1,0:T(8,128)(2,1)}), bf16[16,40,2560]{2,1,0:T(8,128)(2,1)}, u32[]{:S(2)}, u32[]{:S(2)}) async-start(bf16[16,40,2560]{2,1,0:T(8,128)(2,1)} %bitcast.168), calls=%async_computation | async-start | bytes 6553600 | tf_op jit(solution)/shard_map/while/body/eval_jaxpr/all_to_all | solution.py:109
  295.1 52.6 %all-to-all-start.1 = ((bf16[16,40,2560]{2,1,0:T(8,128)(2,1)}), bf16[16,40,2560]{2,1,0:T(8,128)(2,1)S(1)}, u32[]{:S(2)}, u32[]{:S(2)}) async-start(bf16[16,40,2560]{2,1,0:T(8,128)(2,1)} %bitcast.167), calls=%async_computation.1 | async-start | bytes 6553600 | tf_op jit(solution)/shard_map/while/body/eval_jaxpr/all_to_all | solution.py:108
  349.6 52.6 %all-to-all-start.2 = ((bf16[16,40,2560]{2,1,0:T(8,128)(2,1)}), bf16[16,40,2560]{2,1,0:T(8,128)(2,1)S(1)}, u32[]{:S(2)}, u32[]{:S(2)}) async-start(bf16[16,40,2560]{2,1,0:T(8,128)(2,1)} %copy-done), calls=%async_computation.2 | async-start | bytes 6553600 | tf_op jit(solution)/shard_map/while/body/eval_jaxpr/all_to_all | solution.py:112
  408.2 49.8 %copy-start.10 = (f32[2,64,1]{1,2,0:T(1,128)S(1)}, f32[2,64,1]{1,2,0:T(1,128)}, u32[]{:S(2)}) copy-start(f32[2,64,1]{1,2,0:T(1,128)} %copy-done.9) | copy-start | bytes 1540 | tf_op jit(solution)/shard_map/while
  411.1 46.9 %collective-permute-start = (bf16[64,2560]{1,0:T(8,128)(2,1)S(1)}, bf16[64,2560]{1,0:T(8,128)(2,1)S(1)}, u32[]{:S(2)}, u32[]{:S(2)}) collective-permute-start(bf16[64,2560]{1,0:T(8,128)(2,1)S(1)} %get-tuple-element.529), channel_id=1, source_target_pairs={{0,112},{16,0},{32,16},{48,32},{64,48},{80,64},{96,80},{112,96},{1... | collective-permute-start | bytes 983048 | tf_op jit(solution)/shard_map/while/body/eval_jaxpr/ppermute | solution.py:11
  458.0 119.1 %copy-start.9 = (f32[2,64,1]{1,2,0:T(1,128)}, f32[2,64,1]{1,2,0:T(1,128)S(1)}, u32[]{:S(2)}) copy-start(f32[2,64,1]{1,2,0:T(1,128)S(1)} %get-tuple-element.579) | copy-start | bytes 1540 | tf_op jit(solution)/shard_map/while
  464.2 52.8 %all-to-all-start = ((bf16[16,40,2560]{2,1,0:T(8,128)(2,1)}), bf16[16,40,2560]{2,1,0:T(8,128)(2,1)}, u32[]{:S(2)}, u32[]{:S(2)}) async-start(bf16[16,40,2560]{2,1,0:T(8,128)(2,1)} %bitcast.168), calls=%async_computation | async-start | bytes 6553600 | tf_op jit(solution)/shard_map/while/body/eval_jaxpr/all_to_all | solution.py:109
  516.9 52.6 %all-to-all-start.1 = ((bf16[16,40,2560]{2,1,0:T(8,128)(2,1)}), bf16[16,40,2560]{2,1,0:T(8,128)(2,1)S(1)}, u32[]{:S(2)}, u32[]{:S(2)}) async-start(bf16[16,40,2560]{2,1,0:T(8,128)(2,1)} %bitcast.167), calls=%async_computation.1 | async-start | bytes 6553600 | tf_op jit(solution)/shard_map/while/body/eval_jaxpr/all_to_all | solution.py:108
  571.5 52.6 %all-to-all-start.2 = ((bf16[16,40,2560]{2,1,0:T(8,128)(2,1)}), bf16[16,40,2560]{2,1,0:T(8,128)(2,1)S(1)}, u32[]{:S(2)}, u32[]{:S(2)}) async-start(bf16[16,40,2560]{2,1,0:T(8,128)(2,1)} %copy-done), calls=%async_computation.2 | async-start | bytes 6553600 | tf_op jit(solution)/shard_map/while/body/eval_jaxpr/all_to_all | solution.py:112
  633.0 12.5 collective-permute-start
  645.5 119.1 %copy-start.9 = (f32[2,64,1]{1,2,0:T(1,128)}, f32[2,64,1]{1,2,0:T(1,128)S(1)}, u32[]{:S(2)}) copy-start(f32[2,64,1]{1,2,0:T(1,128)S(1)} %get-tuple-element.579) | copy-start | bytes 1540 | tf_op jit(solution)/shard_map/while
  651.6 52.8 %all-to-all-start = ((bf16[16,40,2560]{2,1,0:T(8,128)(2,1)}), bf16[16,40,2560]{2,1,0:T(8,128)(2,1)}, u32[]{:S(2)}, u32[]{:S(2)}) async-start(bf16[16,40,2560]{2,1,0:T(8,128)(2,1)} %bitcast.168), calls=%async_computation | async-start | bytes 6553600 | tf_op jit(solution)/shard_map/while/body/eval_jaxpr/all_to_all | solution.py:109
  704.4 52.6 %all-to-all-start.1 = ((bf16[16,40,2560]{2,1,0:T(8,128)(2,1)}), bf16[16,40,2560]{2,1,0:T(8,128)(2,1)S(1)}, u32[]{:S(2)}, u32[]{:S(2)}) async-start(bf16[16,40,2560]{2,1,0:T(8,128)(2,1)} %bitcast.167), calls=%async_computation.1 | async-start | bytes 6553600 | tf_op jit(solution)/shard_map/while/body/eval_jaxpr/all_to_all | solution.py:108
  758.9 52.6 %all-to-all-start.2 = ((bf16[16,40,2560]{2,1,0:T(8,128)(2,1)}), bf16[16,40,2560]{2,1,0:T(8,128)(2,1)S(1)}, u32[]{:S(2)}, u32[]{:S(2)}) async-start(bf16[16,40,2560]{2,1,0:T(8,128)(2,1)} %copy-done), calls=%async_computation.2 | async-start | bytes 6553600 | tf_op jit(solution)/shard_map/while/body/eval_jaxpr/all_to_all | solution.py:112
  820.4 41.4 %collective-permute-start = (bf16[64,2560]{1,0:T(8,128)(2,1)S(1)}, bf16[64,2560]{1,0:T(8,128)(2,1)S(1)}, u32[]{:S(2)}, u32[]{:S(2)}) collective-permute-start(bf16[64,2560]{1,0:T(8,128)(2,1)S(1)} %get-tuple-element.529), channel_id=1, source_target_pairs={{0,112},{16,0},{32,16},{48,32},{64,48},{80,64},{96,80},{112,96},{1... | collective-permute-start | bytes 983048 | tf_op jit(solution)/shard_map/while/body/eval_jaxpr/ppermute | solution.py:11
  861.8 119.1 %copy-start.9 = (f32[2,64,1]{1,2,0:T(1,128)}, f32[2,64,1]{1,2,0:T(1,128)S(1)}, u32[]{:S(2)}) copy-start(f32[2,64,1]{1,2,0:T(1,128)S(1)} %get-tuple-element.579) | copy-start | bytes 1540 | tf_op jit(solution)/shard_map/while
  867.9 52.8 %all-to-all-start = ((bf16[16,40,2560]{2,1,0:T(8,128)(2,1)}), bf16[16,40,2560]{2,1,0:T(8,128)(2,1)}, u32[]{:S(2)}, u32[]{:S(2)}) async-start(bf16[16,40,2560]{2,1,0:T(8,128)(2,1)} %bitcast.168), calls=%async_computation | async-start | bytes 6553600 | tf_op jit(solution)/shard_map/while/body/eval_jaxpr/all_to_all | solution.py:109
  920.7 52.6 %all-to-all-start.1 = ((bf16[16,40,2560]{2,1,0:T(8,128)(2,1)}), bf16[16,40,2560]{2,1,0:T(8,128)(2,1)S(1)}, u32[]{:S(2)}, u32[]{:S(2)}) async-start(bf16[16,40,2560]{2,1,0:T(8,128)(2,1)} %bitcast.167), calls=%async_computation.1 | async-start | bytes 6553600 | tf_op jit(solution)/shard_map/while/body/eval_jaxpr/all_to_all | solution.py:108
  975.3 52.6 %all-to-all-start.2 = ((bf16[16,40,2560]{2,1,0:T(8,128)(2,1)}), bf16[16,40,2560]{2,1,0:T(8,128)(2,1)S(1)}, u32[]{:S(2)}, u32[]{:S(2)}) async-start(bf16[16,40,2560]{2,1,0:T(8,128)(2,1)} %copy-done), calls=%async_computation.2 | async-start | bytes 6553600 | tf_op jit(solution)/shard_map/while/body/eval_jaxpr/all_to_all | solution.py:112
  1036.8 12.5 collective-permute-start
  1049.2 119.1 %copy-start.9 = (f32[2,64,1]{1,2,0:T(1,128)}, f32[2,64,1]{1,2,0:T(1,128)S(1)}, u32[]{:S(2)}) copy-start(f32[2,64,1]{1,2,0:T(1,128)S(1)} %get-tuple-element.579) | copy-start | bytes 1540 | tf_op jit(solution)/shard_map/while
  1055.4 52.8 %all-to-all-start = ((bf16[16,40,2560]{2,1,0:T(8,128)(2,1)}), bf16[16,40,2560]{2,1,0:T(8,128)(2,1)}, u32[]{:S(2)}, u32[]{:S(2)}) async-start(bf16[16,40,2560]{2,1,0:T(8,128)(2,1)} %bitcast.168), calls=%async_computation | async-start | bytes 6553600 | tf_op jit(solution)/shard_map/while/body/eval_jaxpr/all_to_all | solution.py:109
  1108.1 52.6 %all-to-all-start.1 = ((bf16[16,40,2560]{2,1,0:T(8,128)(2,1)}), bf16[16,40,2560]{2,1,0:T(8,128)(2,1)S(1)}, u32[]{:S(2)}, u32[]{:S(2)}) async-start(bf16[16,40,2560]{2,1,0:T(8,128)(2,1)} %bitcast.167), calls=%async_computation.1 | async-start | bytes 6553600 | tf_op jit(solution)/shard_map/while/body/eval_jaxpr/all_to_all | solution.py:108
  1162.7 52.6 %all-to-all-start.2 = ((bf16[16,40,2560]{2,1,0:T(8,128)(2,1)}), bf16[16,40,2560]{2,1,0:T(8,128)(2,1)S(1)}, u32[]{:S(2)}, u32[]{:S(2)}) async-start(bf16[16,40,2560]{2,1,0:T(8,128)(2,1)} %copy-done), calls=%async_computation.2 | async-start | bytes 6553600 | tf_op jit(solution)/shard_map/while/body/eval_jaxpr/all_to_all | solution.py:112
  1224.2 42.3 %collective-permute-start = (bf16[64,2560]{1,0:T(8,128)(2,1)S(1)}, bf16[64,2560]{1,0:T(8,128)(2,1)S(1)}, u32[]{:S(2)}, u32[]{:S(2)}) collective-permute-start(bf16[64,2560]{1,0:T(8,128)(2,1)S(1)} %get-tuple-element.529), channel_id=1, source_target_pairs={{0,112},{16,0},{32,16},{48,32},{64,48},{80,64},{96,80},{112,96},{1... | collective-permute-start | bytes 983048 | tf_op jit(solution)/shard_map/while/body/eval_jaxpr/ppermute | solution.py:11
  1266.5 119.1 %copy-start.9 = (f32[2,64,1]{1,2,0:T(1,128)}, f32[2,64,1]{1,2,0:T(1,128)S(1)}, u32[]{:S(2)}) copy-start(f32[2,64,1]{1,2,0:T(1,128)S(1)} %get-tuple-element.579) | copy-start | bytes 1540 | tf_op jit(solution)/shard_map/while
  1272.6 52.8 %all-to-all-start = ((bf16[16,40,2560]{2,1,0:T(8,128)(2,1)}), bf16[16,40,2560]{2,1,0:T(8,128)(2,1)}, u32[]{:S(2)}, u32[]{:S(2)}) async-start(bf16[16,40,2560]{2,1,0:T(8,128)(2,1)} %bitcast.168), calls=%async_computation | async-start | bytes 6553600 | tf_op jit(solution)/shard_map/while/body/eval_jaxpr/all_to_all | solution.py:109
  1325.4 52.6 %all-to-all-start.1 = ((bf16[16,40,2560]{2,1,0:T(8,128)(2,1)}), bf16[16,40,2560]{2,1,0:T(8,128)(2,1)S(1)}, u32[]{:S(2)}, u32[]{:S(2)}) async-start(bf16[16,40,2560]{2,1,0:T(8,128)(2,1)} %bitcast.167), calls=%async_computation.1 | async-start | bytes 6553600 | tf_op jit(solution)/shard_map/while/body/eval_jaxpr/all_to_all | solution.py:108
  1379.9 52.6 %all-to-all-start.2 = ((bf16[16,40,2560]{2,1,0:T(8,128)(2,1)}), bf16[16,40,2560]{2,1,0:T(8,128)(2,1)S(1)}, u32[]{:S(2)}, u32[]{:S(2)}) async-start(bf16[16,40,2560]{2,1,0:T(8,128)(2,1)} %copy-done), calls=%async_computation.2 | async-start | bytes 6553600 | tf_op jit(solution)/shard_map/while/body/eval_jaxpr/all_to_all | solution.py:112
  1438.6 116.7 %copy-start.10 = (f32[2,64,1]{1,2,0:T(1,128)S(1)}, f32[2,64,1]{1,2,0:T(1,128)}, u32[]{:S(2)}) copy-start(f32[2,64,1]{1,2,0:T(1,128)} %copy-done.9) | copy-start | bytes 1540 | tf_op jit(solution)/shard_map/while
  1441.4 113.8 %copy-start.5 = (bf16[2,64,2560]{2,1,0:T(8,128)(2,1)}, bf16[2,64,2560]{2,1,0:T(8,128)(2,1)S(1)}, u32[]{:S(2)}) copy-start(bf16[2,64,2560]{2,1,0:T(8,128)(2,1)S(1)} %get-tuple-element.575) | copy-start | bytes 1966084 | tf_op jit(solution)/shard_map/while
  1441.4 113.8 %collective-permute-start = (bf16[64,2560]{1,0:T(8,128)(2,1)S(1)}, bf16[64,2560]{1,0:T(8,128)(2,1)S(1)}, u32[]{:S(2)}, u32[]{:S(2)}) collective-permute-start(bf16[64,2560]{1,0:T(8,128)(2,1)S(1)} %get-tuple-element.529), channel_id=1, source_target_pairs={{0,112},{16,0},{32,16},{48,32},{64,48},{80,64},{96,80},{112,96},{1... | collective-permute-start | bytes 983048 | tf_op jit(solution)/shard_map/while/body/eval_jaxpr/ppermute | solution.py:11
  1555.2 153.5 %copy-start.9 = (f32[2,64,1]{1,2,0:T(1,128)}, f32[2,64,1]{1,2,0:T(1,128)S(1)}, u32[]{:S(2)}) copy-start(f32[2,64,1]{1,2,0:T(1,128)S(1)} %get-tuple-element.579) | copy-start | bytes 1540 | tf_op jit(solution)/shard_map/while
  1561.4 52.8 %all-to-all-start = ((bf16[16,40,2560]{2,1,0:T(8,128)(2,1)}), bf16[16,40,2560]{2,1,0:T(8,128)(2,1)}, u32[]{:S(2)}, u32[]{:S(2)}) async-start(bf16[16,40,2560]{2,1,0:T(8,128)(2,1)} %bitcast.168), calls=%async_computation | async-start | bytes 6553600 | tf_op jit(solution)/shard_map/while/body/eval_jaxpr/all_to_all | solution.py:109
  1614.1 52.6 %all-to-all-start.1 = ((bf16[16,40,2560]{2,1,0:T(8,128)(2,1)}), bf16[16,40,2560]{2,1,0:T(8,128)(2,1)S(1)}, u32[]{:S(2)}, u32[]{:S(2)}) async-start(bf16[16,40,2560]{2,1,0:T(8,128)(2,1)} %bitcast.167), calls=%async_computation.1 | async-start | bytes 6553600 | tf_op jit(solution)/shard_map/while/body/eval_jaxpr/all_to_all | solution.py:108
  1703.1 52.6 %all-to-all-start.2 = ((bf16[16,40,2560]{2,1,0:T(8,128)(2,1)}), bf16[16,40,2560]{2,1,0:T(8,128)(2,1)S(1)}, u32[]{:S(2)}, u32[]{:S(2)}) async-start(bf16[16,40,2560]{2,1,0:T(8,128)(2,1)} %copy-done), calls=%async_computation.2 | async-start | bytes 6553600 | tf_op jit(solution)/shard_map/while/body/eval_jaxpr/all_to_all | solution.py:112
  1764.6 13.7 collective-permute-start
  1778.3 153.5 %copy-start.9 = (f32[2,64,1]{1,2,0:T(1,128)}, f32[2,64,1]{1,2,0:T(1,128)S(1)}, u32[]{:S(2)}) copy-start(f32[2,64,1]{1,2,0:T(1,128)S(1)} %get-tuple-element.579) | copy-start | bytes 1540 | tf_op jit(solution)/shard_map/while
  1784.4 52.8 %all-to-all-start = ((bf16[16,40,2560]{2,1,0:T(8,128)(2,1)}), bf16[16,40,2560]{2,1,0:T(8,128)(2,1)}, u32[]{:S(2)}, u32[]{:S(2)}) async-start(bf16[16,40,2560]{2,1,0:T(8,128)(2,1)} %bitcast.168), calls=%async_computation | async-start | bytes 6553600 | tf_op jit(solution)/shard_map/while/body/eval_jaxpr/all_to_all | solution.py:109
  1837.2 52.6 %all-to-all-start.1 = ((bf16[16,40,2560]{2,1,0:T(8,128)(2,1)}), bf16[16,40,2560]{2,1,0:T(8,128)(2,1)S(1)}, u32[]{:S(2)}, u32[]{:S(2)}) async-start(bf16[16,40,2560]{2,1,0:T(8,128)(2,1)} %bitcast.167), calls=%async_computation.1 | async-start | bytes 6553600 | tf_op jit(solution)/shard_map/while/body/eval_jaxpr/all_to_all | solution.py:108
  1926.1 52.6 %all-to-all-start.2 = ((bf16[16,40,2560]{2,1,0:T(8,128)(2,1)}), bf16[16,40,2560]{2,1,0:T(8,128)(2,1)S(1)}, u32[]{:S(2)}, u32[]{:S(2)}) async-start(bf16[16,40,2560]{2,1,0:T(8,128)(2,1)} %copy-done), calls=%async_computation.2 | async-start | bytes 6553600 | tf_op jit(solution)/shard_map/while/body/eval_jaxpr/all_to_all | solution.py:112
  1987.6 11.6 collective-permute-start
  (65 other events, 570.5 us)
where the time goes:
time: 2000 us
  waiting for transfers between devices  1400 us (70%)
  starting transfers between devices  306 us (15%)
  local copies, waits for them, and re-layouts  174 us (9%)
  matrix products  89.1 us (4%)
  other arithmetic  23.1 us (1%)
    all_to_all x9, waiting for transfers between devices, tick(): lax.all_to_all(row_buffer, 'expert', split_axis=0, concat_axis=0, tiled=T...  425 us
    all_to_all x9, waiting for transfers between devices, tick(): lax.all_to_all(result, 'expert', split_axis=0, concat_axis=0, tiled=True)  423 us
    all_to_all x9, waiting for transfers between devices, tick(): lax.all_to_all(grad_buffer, 'expert', split_axis=0, concat_axis=0, tiled=...  378 us
    ppermute x9, waiting for transfers between devices, from_behind(): lax.ppermute(array, axis, [(i, (i + by) % count) for i in range(count)])  179 us
    ppermute x9, starting transfers between devices, from_behind(): lax.ppermute(array, axis, [(i, (i + by) % count) for i in range(count)])  159 us
    gather x18, local copies, waits for them, and re-layouts, fill_buffer(): return padded[table].reshape(experts, capacity, width)  77.8 us
    all_to_all x9, starting transfers between devices, tick(): lax.all_to_all(grad_buffer, 'expert', split_axis=0, concat_axis=0, tiled=...  49 us
    all_to_all x9, starting transfers between devices, tick(): lax.all_to_all(row_buffer, 'expert', split_axis=0, concat_axis=0, tiled=T...  48.9 us
  transfers between devices with their start and end apart: 36, of which 36 were waited for; matrix products, arithmetic and copies ran while one was open for 2% of the time, Pallas kernels for 0%

commit v1 on v0

v1 whole, which is shorter than its diff:
```python
import jax
import jax.numpy as jnp
from jax import lax
from jax.experimental import pallas as pl
from jax.experimental.pallas import tpu as pltpu
from jax.sharding import PartitionSpec as P

EPSILON = 1e-06
ROWS = 16
NT = (((1,), (1,)), ((), ()))
NN = (((1,), (0,)), ((), ()))
F32 = jnp.float32
BF16 = jnp.bfloat16
MESH = pl.DeviceIdType.MESH
PEERS = 8
COLS = 512


def opposite(j):
    dx, dy = divmod(j, 4)
    return dx * 4 + (4 - dy) % 4


def wait_bytes(ref, sem):
    pltpu.make_async_copy(ref, ref, sem).wait()


def window_kernel(
    x_ref, gain_ref, routing_ref, weight_ref, gate_hbm, up_hbm, down_hbm, top_hbm, out_ref,
    gate, up, down, factors, xb, cb, ag, rs_out, rs_in, hid,
    local_sem, wsend, wrecv, top_sem, xsend, xrecv, csend, crecv,
    gsend, grecv, rsend, rrecv, lsend, lrecv,
):
    chunks = x_ref.shape[0]
    width = x_ref.shape[2]
    section = lax.axis_index("section")
    me = lax.axis_index("expert")
    sections = lax.axis_size("section")
    depth = lax.rem(section + sections // 2, sections)
    below = lax.rem(section + sections - 1, sections)
    above = lax.rem(section + 1, sections)
    core = lax.rem(me, 2)
    row = lax.rem(me // 2, 4)
    side = me // 8
    partner = me + 1 - 2 * core
    is_top = depth == sections - 1

    def peer(j):
        dx, dy = divmod(j, 4)
        return lax.rem(side + dx, 2) * 8 + lax.rem(row + dy, 4) * 2 + core

    pairs = [(gate_hbm, gate), (up_hbm, up), (down_hbm, down)]
    for n, (src, dst) in enumerate(pairs):
        pltpu.make_async_copy(src, dst.at[0], local_sem.at[n]).start()

    barrier = pltpu.get_barrier_semaphore()
    for j in range(1, PEERS):
        pl.semaphore_signal(barrier, inc=1, device_id=(section, peer(j)), device_id_type=MESH)
    pl.semaphore_signal(barrier, inc=1, device_id=(section, partner), device_id_type=MESH)
    pl.semaphore_signal(barrier, inc=1, device_id=(below, me), device_id_type=MESH)
    pl.semaphore_signal(barrier, inc=1, device_id=(above, me), device_id_type=MESH)

    @pl.when(is_top)
    def _():
        for c in range(chunks):
            pltpu.make_async_copy(top_hbm.at[c], ag.at[c, 0], top_sem.at[c]).start()

    gain = gain_ref[...]

    def local_part(c, _):
        x = x_ref[c].astype(F32)
        scale = lax.rsqrt(jnp.mean(x * x, axis=-1, keepdims=True) + EPSILON)
        xb[c, 0] = (x * scale * gain).astype(BF16)
        chosen = routing_ref[c]
        weights = weight_ref[c]
        lanes = lax.broadcasted_iota(jnp.int32, (ROWS, 128), 1)
        coef = jnp.zeros((ROWS, 128), F32)
        for k in range(chosen.shape[1]):
            coef = coef + jnp.where(lanes == chosen[:, k : k + 1], weights[:, k : k + 1], 0.0)
        cb[c, 0] = coef
        return 0

    lax.fori_loop(0, chunks, local_part, 0)
    pl.semaphore_wait(barrier, PEERS + 2)

    weight_copies = []
    for n, (src, dst) in enumerate(pairs):
        copy = pltpu.make_async_remote_copy(
            src_ref=src, dst_ref=dst.at[1], send_sem=wsend.at[n], recv_sem=wrecv.at[n],
            device_id=(section, partner), device_id_type=MESH,
        )
        copy.start()
        weight_copies.append(copy)

    def spread(buf, c, send, recv):
        for j in range(1, PEERS):
            pltpu.make_async_remote_copy(
                src_ref=buf.at[c, 0], dst_ref=buf.at[c, opposite(j)],
                send_sem=send.at[c], recv_sem=recv.at[c],
                device_id=(section, peer(j)), device_id_type=MESH,
            ).start()

    def send_inputs(c, _):
        spread(cb, c, csend, crecv)
        spread(xb, c, xsend, xrecv)

        @pl.when(is_top)
        def _():
            wait_bytes(ag.at[c, 0], top_sem.at[c])
            spread(ag, c, gsend, grecv)

        return 0

    lax.fori_loop(0, chunks, send_inputs, 0)

    for n, (src, dst) in enumerate(pairs):
        pltpu.make_async_copy(src, dst.at[0], local_sem.at[n]).wait()
        weight_copies[n].wait_recv()

    others = pl.ds(1, PEERS - 1)

    def prepare(c):
        wait_bytes(cb.at[c, others], crecv.at[c])
        wait_bytes(xb.at[c, others], xrecv.at[c])
        x = xb[c].reshape(PEERS * ROWS, width)
        coef = cb[c].reshape(PEERS * ROWS, 128)
        lanes = lax.broadcasted_iota(jnp.int32, coef.shape, 1)
        for n, owner in enumerate((me, partner)):
            part = jnp.sum(jnp.where(lanes == owner, coef, 0.0), axis=-1, keepdims=True)
            pre_gate = lax.dot_general(x, gate[n], NN, preferred_element_type=F32)
            pre_up = lax.dot_general(x, up[n], NN, preferred_element_type=F32)
            q = jax.nn.sigmoid(pre_gate)
            factors[c, n, 0] = (part * pre_up * q * (1.0 + pre_gate * (1.0 - q))).astype(BF16)
            factors[c, n, 1] = (part * pre_gate * q).astype(BF16)

    def start_gather(c):
        wait_bytes(ag.at[c, 0], lrecv.at[c])
        spread(ag, c, gsend, grecv)

    def compute(c):
        wait_bytes(ag.at[c, others], grecv.at[c])
        g = ag[c].reshape(PEERS * ROWS, width)
        for n in range(2):
            hidden = lax.dot_general(g, down[n], NT, preferred_element_type=F32)
            hid[n, 0] = (hidden * factors[c, n, 0].astype(F32)).astype(BF16)
            hid[n, 1] = (hidden * factors[c, n, 1].astype(F32)).astype(BF16)
        for col in range(0, width, COLS):
            total = jnp.zeros((PEERS * ROWS, COLS), F32)
            for n in range(2):
                for t, mat in enumerate((gate, up)):
                    total = total + lax.dot_general(
                        hid[n, t], mat[n, col : col + COLS, :], NT, preferred_element_type=F32
                    )
            rs_out[c, :, :, col : col + COLS] = total.astype(BF16).reshape(PEERS, ROWS, COLS)
        for j in range(1, PEERS):
            pltpu.make_async_remote_copy(
                src_ref=rs_out.at[c, j], dst_ref=rs_in.at[c, opposite(j)],
                send_sem=rsend.at[c], recv_sem=rrecv.at[c],
                device_id=(section, peer(j)), device_id_type=MESH,
            ).start()

    def relay(c):
        return pltpu.make_async_remote_copy(
            src_ref=out_ref.at[c], dst_ref=ag.at[c, 0], send_sem=lsend.at[c], recv_sem=lrecv.at[c],
            device_id=(below, me), device_id_type=MESH,
        )

    def finish(c):
        x = x_ref[c].astype(F32)
        scale = lax.rsqrt(jnp.mean(x * x, axis=-1, keepdims=True) + EPSILON)
        wait_bytes(rs_in.at[c, others], rrecv.at[c])
        dy = rs_out[c, 0].astype(F32)
        for j in range(1, PEERS):
            dy = dy + rs_in[c, j].astype(F32)
        scaled = gain * dy
        change = scale * scaled - x * scale**3 * jnp.mean(x * scaled, axis=-1, keepdims=True)
        out_ref[c] = (ag[c, 0].astype(F32) + change).astype(BF16)

        @pl.when(depth > 0)
        def _():
            relay(c).start()

    @pl.when(jnp.logical_not(is_top))
    def _():
        def body(c, _):
            prepare(c)
            return 0

        lax.fori_loop(0, chunks, body, 0)
        start_gather(0)

    def main(c, _):
        @pl.when(is_top)
        def _():
            prepare(c)

        compute(c)

        @pl.when(jnp.logical_and(jnp.logical_not(is_top), c + 1 < chunks))
        def _():
            start_gather(c + 1)

        finish(c)
        return 0

    lax.fori_loop(0, chunks, main, 0)

    def drain(c, _):
        wait_bytes(cb.at[c, others], csend.at[c])
        wait_bytes(xb.at[c, others], xsend.at[c])
        wait_bytes(ag.at[c, others], gsend.at[c])
        wait_bytes(rs_in.at[c, others], rsend.at[c])

        @pl.when(depth > 0)
        def _():
            wait_bytes(out_ref.at[c], lsend.at[c])

        return 0

    lax.fori_loop(0, chunks, drain, 0)
    for copy in weight_copies:
        copy.wait_send()


def per_device(layer_inputs, norm_gain, routing, route_weight, w_gate, w_up, w_down, top_grad):
    _, micro_count, token_count, width = layer_inputs.shape
    top_count = routing.shape[3]
    hidden = w_gate.shape[3]
    chunks = micro_count * token_count // ROWS
    vmem = pl.BlockSpec(memory_space=pltpu.VMEM)
    anyspace = pl.BlockSpec(memory_space=pl.ANY)
    dma = pltpu.SemaphoreType.DMA
    block = (chunks, PEERS, ROWS, width)
    out = pl.pallas_call(
        window_kernel,
        out_shape=jax.ShapeDtypeStruct((chunks, ROWS, width), BF16),
        in_specs=[vmem] * 4 + [anyspace] * 4,
        out_specs=vmem,
        scratch_shapes=[
            pltpu.VMEM((2, width, hidden), BF16),
            pltpu.VMEM((2, width, hidden), BF16),
            pltpu.VMEM((2, hidden, width), BF16),
            pltpu.VMEM((chunks, 2, 2, PEERS * ROWS, hidden), BF16),
            pltpu.VMEM(block, BF16),
            pltpu.VMEM((chunks, PEERS, ROWS, 128), F32),
            pltpu.VMEM(block, BF16),
            pltpu.VMEM(block, BF16),
            pltpu.VMEM(block, BF16),
            pltpu.VMEM((2, 2, PEERS * ROWS, hidden), BF16),
        ]
        + [dma((3,))] * 3
        + [dma((chunks,))] * 11,
        compiler_params=pltpu.CompilerParams(
            collective_id=0, has_side_effects=True, vmem_limit_bytes=67043328
        ),
    )(
        layer_inputs.reshape(chunks, ROWS, width),
        norm_gain,
        routing.reshape(chunks, ROWS, top_count),
        route_weight.reshape(chunks, ROWS, top_count),
        w_gate[0, 0],
        w_up[0, 0],
        w_down[0, 0],
        top_grad.reshape(chunks, ROWS, width),
    )
    return out.reshape(layer_inputs.shape)


def solution(mesh):
    placed = (
        P("section", None, "expert", None),
        P("section", None),
        P("section", None, "expert", None),
        P("section", None, "expert", None),
        P("section", "expert", None, None),
        P("section", "expert", None, None),
        P("section", "expert", None, None),
        P(None, "expert", None),
    )
    return jax.shard_map(
        per_device,
        mesh=mesh,
        in_specs=placed,
        out_specs=P("section", None, "expert", None),
        check_vma=False,
    )
```

time: 2000 us -> 524 us (0.26)
  waiting for transfers between devices: 1400 us -> 0 us
  Pallas kernels: 0 us -> 517 us
  starting transfers between devices: 306 us -> 0 us
  local copies, waits for them, and re-layouts: 174 us -> 4.81 us
  matrix products: 89.1 us -> 0 us
  other arithmetic: 23.1 us -> 0 us
    all_to_all x27 -> x0, waiting for transfers between devices: 1230 us -> none  [the longest x9 425 us: tick(): lax.all_to_all(row_buffer, 'expert', split_axis=0, concat_axis=0, tiled=T...]
    pallas_call x0 -> x1, Pallas kernels: none -> 517 us  [per_device(): pl.pallas_call(window_kernel, out_shape=jax.ShapeDtypeStruct((chunks, ROW...]
    ppermute x9 -> x0, waiting for transfers between devices: 179 us -> none  [from_behind(): lax.ppermute(array, axis, [(i, (i + by) % count) for i in range(count)])]
    ppermute x9 -> x0, starting transfers between devices: 159 us -> none  [from_behind(): lax.ppermute(array, axis, [(i, (i + by) % count) for i in range(count)])]
    all_to_all x27 -> x0, starting transfers between devices: 147 us -> none  [the longest x9 49 us: tick(): lax.all_to_all(grad_buffer, 'expert', split_axis=0, concat_axis=0, tiled=...]
    gather x27 -> x0, local copies, waits for them, and re-layouts: 107 us -> none  [the longest x18 77.8 us: fill_buffer(): return padded[table].reshape(experts, capacity, width)]
    dot_general x17 -> x0, matrix products: 89.1 us -> none  [the longest x2 28.7 us: finish(): jnp.einsum('nch,dh->ncd', grad_gate, gate_mat, preferred_element_type=jnp...]
    reshape x9 -> x0, local copies, waits for them, and re-layouts: 23.5 us -> none  [tick(): picked = picked.reshape(token_count, top_count, width).astype(jnp.float32)]
  transfers between devices with their start and end apart: 36 -> 0, of which waited for: 36 -> 0; matrix products, arithmetic and copies ran while one was open for 2% -> 0% of each run, Pallas kernels for 0% -> 0%
where the time goes in v1:
time: 524 us; the launch traced here: 522 us
  Pallas kernels  517 us (99%)
    pallas_call x1, Pallas kernels, per_device(): pl.pallas_call(window_kernel, out_shape=jax.ShapeDtypeStruct((chunks, ROW...  517 us

profile of v1, /device:TPU:90, one launch (start us, length us, event | category | flops | bytes accessed | tf_op | source)
XLA Modules:
  0.0 522.2 jit_solution(7169687724039370525)
XLA Ops:
  0.0 1.4 copy.9
  1.4 1.4 copy.10
  2.8 517.4 %shard_map.82 = bf16[8,16,2560]{2,1,0:T(8,128)(2,1)} custom-call(bf16[8,16,2560]{2,1,0:T(8,128)(2,1)} %bitcast.12, f32[1,2560]{1,0:T(1,128)} %gain_ref.1, s32[8,16,6]{2,1,0:T(8,128)} %bitcast.14, f32[8,16,6]{2,1,0:T(8,128)} %bitcast.15, bf16[2560,768]{1,0:T(8,128)(2,1)} %bitcast.8, bf16[2560,768]{1,0:T(8,128)(2,1)} %bitcast.9, bf16[768,2560]{1,0:T(8,128)(2,1)} %bitcast.10, ...), custom_call_target="tpu_custom_call" | custom-call | tf_op jit(solution)/shard_map/pallas_call | solution.py:234
  520.3 2.0 copy.12
